TPU v7x, 128 devices: a whole 4x4x4 slice. The times are simulated.
128 devices in a mesh: expert: 32 (over z, y, core), helper: 4 (over x).
Axes of the slice: x: 4, y: 4, z: 4, core: 2. Of those that a mesh axis runs over, the one named last changes fastest.
Arguments:
- tokens: bfloat16 [131072, 768], P(('expert', 'helper')), may hold values from -6 to 6
- gate: float32 [131072], P(('expert', 'helper')), may hold values from 0.2 to 1
- expert_ids: int32 [131072, 1], P(('expert', 'helper')), may hold values from 0 to 127; in each aligned block of 1024 rows (0 to 1023, 1024 to 2047, ...) at most 12 rows name the same one
- backup_ids: int32 [131072, 1], P(('expert', 'helper')), may hold values from 0 to 127; in each aligned block of 1024 rows (0 to 1023, 1024 to 2047, ...) at most 12 rows name the same one
- capacity: int32 [128], replicated, may hold values from 2 to 12
- w_in: bfloat16 [128, 768, 3072], P('expert', None, 'helper'), may hold values from -0.21875 to 0.21875
- w_out: bfloat16 [128, 3072, 768], P('expert', 'helper'), may hold values from -0.109375 to 0.109375
Outputs:
- mixed: bfloat16 [131072, 768], P(('expert', 'helper'))
Inputs may be any that keep to these rules, and one draw needn't show every extreme that they name: `expert_ids`: in the rows of one device no expert is the first expert of more than 12 rows; some expert reaches 12. `backup_ids`: in the rows of one device no expert is the backup of more than 12 rows; some expert reaches 12.
All inputs are finite; a program needn't handle non-finite values.
Results may differ from a plain program's by a relative error of at most 0.0095.
Values may be sent and summed in bfloat16 or wider, within the bound.
No kernel may reach another device: no remote copies, remote signals or barrier semaphores. Data moves between devices by JAX's collectives and lax.ppermute only.
A program may use at most 192 MiB of HBM per device.

v0:
```python
import jax
import jax.numpy as jnp
from jax import lax
from jax.sharding import Mesh
from jax.sharding import PartitionSpec as P

EXPERT = ("expert_0", "expert_1", "expert_2")
EXPERT_HELPER = ("expert_0", "expert_1", "expert_2", "helper")


def split_up(array, dim, size):
    dims = array.shape
    parts = array.reshape(*dims[:dim], size, dims[dim] // size, *dims[dim + 1 :])
    return jnp.moveaxis(parts, dim, 0)


def laid_out(parts, dim):
    parts = jnp.moveaxis(parts, 0, dim)
    dims = parts.shape
    return parts.reshape(*dims[:dim], dims[dim] * dims[dim + 1], *dims[dim + 2 :])


def exchange_in_order(parts, axes, order):
    dims = [lax.axis_size(a) for a in axes]
    parts = parts.reshape(*dims, *parts.shape[1:])
    for k in order:
        parts = lax.all_to_all(parts, axes[k], split_axis=k, concat_axis=k, tiled=True)
    return parts.reshape(-1, *parts.shape[len(axes) :])


def core_and_chips(array, groups, order, split_dim, concat_dim):
    size = lax.axis_size(groups[0]) * lax.axis_size(groups[1])
    parts = split_up(array, split_dim, size)
    return laid_out(exchange_in_order(parts, groups, order), concat_dim)


def assign(first, backup, capacity, count, slot):
    columns = jnp.arange(count, dtype=jnp.int32)
    onehot = (first[:, None] == columns[None, :]).astype(jnp.int32)
    rank = jnp.sum((jnp.cumsum(onehot, axis=0) - onehot) * onehot, axis=1)
    limit = jnp.sum(onehot * capacity[None, :], axis=1)
    kept = rank < limit
    spill = (backup[:, None] == columns[None, :]).astype(jnp.int32) * (1 - kept.astype(jnp.int32))[
        :, None
    ]
    spill_rank = jnp.sum((jnp.cumsum(spill, axis=0) - spill) * spill, axis=1)
    final = jnp.where(kept, first, backup)
    slots = jnp.where(kept, rank, slot + spill_rank)
    return (slots, final)


def quarter_term(rows, weight_in, weight_out):
    hidden = jax.nn.relu(jnp.dot(rows, weight_in, preferred_element_type=jnp.float32)).astype(
        jnp.bfloat16
    )
    return jnp.dot(hidden, weight_out, preferred_element_type=jnp.float32)


def on_device(tokens, gate, expert_ids, backup_ids, capacity, w_in, w_out):
    held = w_in.shape[0]
    experts = held * lax.axis_size(EXPERT)
    helpers = lax.axis_size("helper")
    slot = max(6, 3 * tokens.shape[0] // (2 * experts))
    slots, final = assign(expert_ids[:, 0], backup_ids[:, 0], capacity, experts, slot)
    buffer = (
        jnp.zeros((2 * slot, experts, tokens.shape[1]), jnp.bfloat16).at[slots, final].set(tokens)
    )
    arrived = core_and_chips(buffer, (("expert_0", "expert_1"), "expert_2"), (1, 0), 1, 0)
    whole_in, whole_out = (
        lax.all_gather(w_in, "helper", axis=2, tiled=True),
        lax.all_gather(w_out, "helper", axis=1, tiled=True),
    )
    width = whole_in.shape[2] // helpers
    outputs = []
    for expert in range(held):
        total = jnp.zeros((arrived.shape[0], arrived.shape[2]), jnp.float32)
        for quarter in range(helpers):
            part = quarter_term(
                arrived[:, expert],
                whole_in[expert, :, quarter * width : (quarter + 1) * width],
                whole_out[expert, quarter * width : (quarter + 1) * width, :],
            )
            total = total + part.astype(jnp.bfloat16).astype(jnp.float32)
        outputs.append(total.astype(jnp.bfloat16))
    result = jnp.stack(outputs, axis=1)
    returned = core_and_chips(result, (("expert_0", "expert_1"), "expert_2"), (1, 0), 0, 1)
    picked = returned[slots, final]
    return (gate[:, None] * picked.astype(jnp.float32)).astype(jnp.bfloat16)


def solution(mesh):
    torus = Mesh(
        mesh.devices.reshape(4, 4, 2, mesh.shape["helper"]),
        ("expert_0", "expert_1", "expert_2", "helper"),
    )
    in_specs = (
        P(EXPERT_HELPER, None),
        P(EXPERT_HELPER),
        P(EXPERT_HELPER, None),
        P(EXPERT_HELPER, None),
        P(),
        P(EXPERT, None, "helper"),
        P(EXPERT, "helper", None),
    )
    out_specs = P(EXPERT_HELPER, None)
    return jax.shard_map(
        on_device, mesh=torus, in_specs=in_specs, out_specs=out_specs, check_vma=False
    )
```

profile of v0, /device:TPU:0, one launch (start us, length us, event | category | flops | bytes accessed | tf_op | source)
XLA Modules:
  0.0 538.9 jit_solution(8515442696640882063)
XLA Ops:
  6.5 0.7 all-gather.3.cloned.1.call-update
  7.3 0.7 all-gather.5.cloned.1.call-update
  8.0 0.1 copy.32
  8.2 0.1 copy.30
  8.3 0.2 fusion.7
  8.6 0.1 copy.31
  8.7 0.5 select_reduce_fusion
  9.2 0.1 copy.33
  9.3 0.3 fusion.5
  9.7 0.1 copy.34
  9.9 0.5 fusion.2
  10.4 0.1 multiply_reduce_fusion
  10.5 0.1 and_reduce_fusion
  10.6 9.2 %scatter_custom_fusion = bf16[3072,768]{1,0:T(8,128)(2,1)} fusion(s32[1024]{0:T(1024)S(1)} %broadcast_select_fusion, bf16[1024,768]{1,0:T(8,128)(2,1)} %param.7, bf16[]{:T(256)} %constant.31.clone.1), kind=kCustom, calls=%fused_computation.4 | custom fusion | bytes 4719104
  19.9 9.3 %reshape.114 = bf16[24,32,4,768]{3,2,1,0:T(4,128)(2,1)} reshape(bf16[3072,768]{1,0:T(8,128)(2,1)} %scatter_custom_fusion) | data formatting | bytes 9437184 | tf_op jit(solution)/shard_map/reshape | solution.py:13
  29.2 6.7 %copy.35 = bf16[24,32,4,768]{3,0,2,1:T(8,128)(2,1)S(1)} copy(bf16[24,32,4,768]{3,2,1,0:T(4,128)(2,1)} %reshape.114) | data formatting | bytes 9437184 | tf_op jit(solution)/shard_map/reshape | solution.py:13
  35.8 0.3 copy.36
  36.2 7.5 %all_to_all.20 = bf16[16,2,24,4,768]{4,2,0,3,1:T(8,128)(2,1)S(1)} all-to-all(bf16[16,2,24,4,768]{4,2,0,3,1:T(8,128)(2,1)S(1)} %copy.36), channel_id=1, replica_groups=mesh['expert_0'=4,'expert_1'=4,'expert_2'=2,'helper'=4] {'expert_2'}, dimensions={1} | all-to-all | bytes 9437184 | tf_op jit(solution)/shard_map/all_to_all | solution.py:27
  43.7 0.5 copy.37
  44.2 64.8 %all_to_all.21 = bf16[16,2,24,4,768]{4,2,1,3,0:T(8,128)(2,1)S(1)} all-to-all(bf16[16,2,24,4,768]{4,2,1,3,0:T(8,128)(2,1)S(1)} %copy.37), channel_id=1, replica_groups=mesh['expert_0'=4,'expert_1'=4,'expert_2'=2,'helper'=4] {'expert_0','exp..., dimensions={0} | all-to-all | bytes 9437184 | tf_op jit(solution)/shard_map/all_to_all | solution.py:27
  109.0 2.5 copy.38
  111.5 72.4 %all-gather.3.cloned.1.call-done = bf16[4,768,3072]{2,1,0:T(8,128)(2,1)} async-done(((bf16[4,768,768]{2,1,0:T(8,128)(2,1)}), bf16[4,768,3072]{2,1,0:T(8,128)(2,1)}) %all-gather.3.cloned.1.call-update) | async-done | bytes 18874384 | tf_op jit(solution)/shard_map/all_gather | solution.py:70
  183.9 173.4 %all-gather.5.cloned.1.call-done = bf16[4,3072,768]{2,1,0:T(8,128)(2,1)} async-done(((bf16[4,768,768]{2,1,0:T(8,128)(2,1)}), bf16[4,3072,768]{2,1,0:T(8,128)(2,1)}) %all-gather.5.cloned.1.call-update) | async-done | bytes 18874384 | tf_op jit(solution)/shard_map/all_gather | solution.py:71
  357.3 4.1 convolution_convert_fusion.2
  361.4 5.1 convolution_convert_fusion.1
  366.5 5.1 convolution_convert_fusion
  371.7 4.1 convolution_convert_fusion.6
  375.8 5.1 convolution_convert_fusion.5
  380.9 5.2 convolution_convert_fusion.4
  386.1 5.1 convolution_convert_fusion.10
  391.2 5.4 convolution_convert_fusion.9
  396.5 5.2 convolution_convert_fusion.8
  401.7 5.1 convolution_convert_fusion.14
  406.8 5.1 convolution_convert_fusion.13
  411.9 5.1 convolution_convert_fusion.12
  417.1 4.9 add_convert_fusion
  422.0 4.9 add_convert_fusion.1
  426.9 5.2 add_convert_fusion.2
  432.1 6.5 %add_convert_fusion.3 = bf16[768,768]{1,0:T(8,128)(2,1)} fusion(bf16[768,768]{1,0:T(8,128)(2,1)} %convolution_convert_fusion.12, bf16[768,768]{1,0:T(8,128)(2,1)} %convolution_convert_fusion.13, bf16[768,768]{1,0:T(8,128)(2,1)} %convolution_convert_fusion.14, bf16[4,3072,768]{2,1,0:T(8,128)(2,1)} %all-gather.5.cloned.1.call-done, ...), kind=kOutput, calls=%fused_computation.21 | convolution fusion | flops 1818427392 | bytes 8257536 | tf_op jit(solution)/shard_map/dot_general | solution.py:56
  438.7 1.7 pad_maximum_fusion
  440.3 0.3 copy.46
  440.7 7.5 %all_to_all.22 = bf16[16,2,24,4,768]{4,2,0,3,1:T(8,128)(2,1)S(1)} all-to-all(bf16[16,2,24,4,768]{4,2,0,3,1:T(8,128)(2,1)S(1)} %copy.46), channel_id=1, replica_groups=mesh['expert_0'=4,'expert_1'=4,'expert_2'=2,'helper'=4] {'expert_2'}, dimensions={1} | all-to-all | bytes 9437184 | tf_op jit(solution)/shard_map/all_to_all | solution.py:27
  448.2 0.5 copy.43
  448.7 63.6 %all_to_all.23 = bf16[16,2,24,4,768]{4,2,1,3,0:T(8,128)(2,1)S(1)} all-to-all(bf16[16,2,24,4,768]{4,2,1,3,0:T(8,128)(2,1)S(1)} %copy.43), channel_id=1, replica_groups=mesh['expert_0'=4,'expert_1'=4,'expert_2'=2,'helper'=4] {'expert_0','exp..., dimensions={0} | all-to-all | bytes 9437184 | tf_op jit(solution)/shard_map/all_to_all | solution.py:27
  512.3 0.6 copy.44
  512.8 3.2 copy.47
  516.0 14.3 %gather_fusion = bf16[1024,768]{1,0:T(8,128)(2,1)S(1)} fusion(bf16[24,128,768]{2,1,0:T(8,128)(2,1)} %copy.47, s32[1024]{0:T(1024)S(1)} %bitcast.231), kind=kCustom, calls=%fused_computation | custom fusion | bytes 3153920 | tf_op jit(solution)/shard_map/gather | solution.py:87
  530.4 1.5 multiply_convert_fusion
  (26 shorter events, 0.3 us)
Async XLA Ops:
  6.5 177.4 %all-gather.3.cloned.1.call-start = ((), (), s32[]{:S(2)}) async-start(), calls=%async_computation.4 | async-start | bytes 23592960 | tf_op jit(solution)/shard_map/all_gather | solution.py:70
  7.3 0.8 copy-start.1
  7.3 0.9 copy-start
  7.3 350.0 %all-gather.5.cloned.1.call-start = ((), (), s32[]{:S(2)}) async-start(), calls=%async_computation.5 | async-start | bytes 23592960 | tf_op jit(solution)/shard_map/all_gather | solution.py:71
  8.0 0.7 copy-start.3
  8.5 1.9 copy-start.5
  8.6 1.9 copy-start.4
  516.0 14.3 %copy-start.2 = (f32[1024]{0:T(1024)S(1)}, f32[1024]{0:T(1024)}, u32[]{:S(2)}) copy-start(f32[1024]{0:T(1024)} %param.8) | copy-start | bytes 12292
Sparse Core Ops, SparseCore 0:
  9.0 174.8 all-gather.2
  185.6 171.6 all-gather.4
where the time goes:
time: 545 us; the launch traced here: 539 us
  waiting for transfers between devices  247 us (45%)
  blocking collectives  143 us (26%)
  matrix products  81.3 us (15%)
  local copies, waits for them, and re-layouts  48 us (9%)
  between operations  13.9 us (3%)
    all_gather x1, waiting for transfers between devices, on_device(): lax.all_gather(w_out, 'helper', axis=1, tiled=True)  173 us
    all_to_all x4, blocking collectives, exchange_in_order(): lax.all_to_all(parts, axes[k], split_axis=k, concat_axis=k, tiled=True)  143 us
    dot_general x16, matrix products, quarter_term(): return jnp.dot(hidden, weight_out, preferred_element_type=jnp.float32)  81.3 us
    all_gather x1, waiting for transfers between devices, on_device(): lax.all_gather(w_in, 'helper', axis=2, tiled=True)  72.4 us
    reshape x2, local copies, waits for them, and re-layouts, split_up(): parts = array.reshape(*dims[:dim], size, dims[dim] // size, *dims[dim + 1:])  16 us
    gather x1, local copies, waits for them, and re-layouts, on_device(): picked = returned[slots, final]  14.3 us
  transfers between devices with their start and end apart: 2, of which 2 were waited for; matrix products, arithmetic and copies ran while one was open for 6% of the time, Pallas kernels for 0%

commit v1 on v0

--- a/solution.py
+++ b/solution.py
@@ -67,7 +67,9 @@
     )
     arrived = core_and_chips(buffer, (("expert_0", "expert_1"), "expert_2"), (1, 0), 1, 0)
     whole_in, whole_out = (
-        lax.all_gather(w_in, "helper", axis=2, tiled=True),
+        jnp.concatenate(
+            lax.all_to_all(jnp.stack([w_in] * lax.axis_size("helper")), "helper", 0, 0), axis=2
+        ),
         lax.all_gather(w_out, "helper", axis=1, tiled=True),
     )
     width = whole_in.shape[2] // helpers

time: 545 us -> 591 us (1.084)
  blocking collectives: 143 us -> 78.6 us
  waiting for transfers between devices: 247 us -> 305 us
  local copies, waits for them, and re-layouts: 48 us -> 84.8 us
  starting transfers between devices: 0.04 us -> 15.8 us
    all_to_all x0 -> x2, waiting for transfers between devices: none -> 304 us  [the longest x1 240 us: on_device(): lax.all_to_all(jnp.stack([w_in] * lax.axis_size('helper')), 'helper', 0, 0)]
    all_gather x1, waiting for transfers between devices: 173 us -> 0.02 us  [on_device(): lax.all_gather(w_out, 'helper', axis=1, tiled=True)]
    all_gather x1 -> x0, waiting for transfers between devices: 72.4 us -> none  [on_device(): lax.all_gather(w_in, 'helper', axis=2, tiled=True)]
    all_to_all x4 -> x3, blocking collectives: 143 us -> 78.6 us  [exchange_in_order(): lax.all_to_all(parts, axes[k], split_axis=k, concat_axis=k, tiled=True)]
    all_to_all x0 -> x1, local copies, waits for them, and re-layouts: none -> 17.1 us  [on_device(): lax.all_to_all(jnp.stack([w_in] * lax.axis_size('helper')), 'helper', 0, 0)]
    all_to_all x0 -> x2, starting transfers between devices: none -> 15.8 us  [the longest x1 8.31 us: exchange_in_order(): lax.all_to_all(parts, axes[k], split_axis=k, concat_axis=k, tiled=True)]
    another operation x6 -> x7, local copies, waits for them, and re-layouts: 0.22 us -> 8.59 us  [the longest x1 8.37 us: on_device(): jnp.stack([w_in] * lax.axis_size('helper'))]
    unnamed x13 -> x14, local copies, waits for them, and re-layouts: 9.27 us -> 16.1 us
  transfers between devices with their start and end apart: 2 -> 3, of which waited for: 2 -> 2; matrix products, arithmetic and copies ran while one was open for 6% -> 12% of each run, Pallas kernels for 0% -> 0%
where the time goes in v1:
time: 591 us; the launch traced here: 585 us
  waiting for transfers between devices  305 us (52%)
  local copies, waits for them, and re-layouts  84.8 us (14%)
  matrix products  81.7 us (14%)
  blocking collectives  78.6 us (13%)
  starting transfers between devices  15.8 us (3%)
  between operations  14 us (2%)
    all_to_all x1, waiting for transfers between devices, on_device(): lax.all_to_all(jnp.stack([w_in] * lax.axis_size('helper')), 'helper', 0, 0)  240 us
    dot_general x16, matrix products, quarter_term(): return jnp.dot(hidden, weight_out, preferred_element_type=jnp.float32)  81.7 us
    all_to_all x3, blocking collectives, exchange_in_order(): lax.all_to_all(parts, axes[k], split_axis=k, concat_axis=k, tiled=True)  78.6 us
    all_to_all x1, waiting for transfers between devices, exchange_in_order(): lax.all_to_all(parts, axes[k], split_axis=k, concat_axis=k, tiled=True)  64.5 us
    all_to_all x1, local copies, waits for them, and re-layouts, on_device(): lax.all_to_all(jnp.stack([w_in] * lax.axis_size('helper')), 'helper', 0, 0)  17.1 us
    unnamed x14, local copies, waits for them, and re-layouts  16.1 us
    reshape x2, local copies, waits for them, and re-layouts, split_up(): parts = array.reshape(*dims[:dim], size, dims[dim] // size, *dims[dim + 1:])  16 us
    gather x1, local copies, waits for them, and re-layouts, on_device(): picked = returned[slots, final]  14.3 us
  transfers between devices with their start and end apart: 3, of which 2 were waited for; matrix products, arithmetic and copies ran while one was open for 12% of the time, Pallas kernels for 0%

profile of v1, /device:TPU:0, one launch (start us, length us, event | category | flops | bytes accessed | tf_op | source)
XLA Modules:
  0.0 584.6 jit_solution(16576069486488683188)
XLA Ops:
  6.5 0.7 all-gather.2.cloned.1.call-update
  7.3 0.1 copy.33
  7.4 0.2 fusion.7
  7.7 0.1 copy.34
  7.9 0.5 select_reduce_fusion
  8.4 0.1 copy.36
  8.6 0.3 fusion.5
  9.1 0.1 copy.37
  9.2 0.5 fusion.2
  9.9 9.2 %scatter_custom_fusion = bf16[3072,768]{1,0:T(8,128)(2,1)} fusion(s32[1024]{0:T(1024)S(1)} %broadcast_select_fusion, bf16[1024,768]{1,0:T(8,128)(2,1)} %param.7, bf16[]{:T(256)} %constant.31.clone.1), kind=kCustom, calls=%fused_computation.4 | custom fusion | bytes 4719104
  19.2 9.4 %reshape.122 = bf16[24,32,4,768]{3,2,1,0:T(4,128)(2,1)} reshape(bf16[3072,768]{1,0:T(8,128)(2,1)} %scatter_custom_fusion) | data formatting | bytes 9437184 | tf_op jit(solution)/shard_map/reshape | solution.py:13
  28.6 6.7 %copy.38 = bf16[24,32,4,768]{3,0,2,1:T(8,128)(2,1)S(1)} copy(bf16[24,32,4,768]{3,2,1,0:T(4,128)(2,1)} %reshape.122) | data formatting | bytes 9437184 | tf_op jit(solution)/shard_map/reshape | solution.py:13
  35.2 0.3 copy.39
  35.6 7.5 %all_to_all.25 = bf16[16,2,24,4,768]{4,2,0,3,1:T(8,128)(2,1)S(1)} all-to-all(bf16[16,2,24,4,768]{4,2,0,3,1:T(8,128)(2,1)S(1)} %copy.39), channel_id=1, replica_groups=mesh['expert_0'=4,'expert_1'=4,'expert_2'=2,'helper'=4] {'expert_2'}, dimensions={1} | all-to-all | bytes 9437184 | tf_op jit(solution)/shard_map/all_to_all | solution.py:27
  43.1 2.7 copy.40
  45.7 8.3 %all-to-all-start.1 = ((bf16[16,2,24,4,768]{4,2,1,3,0:T(8,128)(2,1)}), bf16[16,2,24,4,768]{4,2,1,3,0:T(8,128)(2,1)}, u32[]{:S(2)}, u32[]{:S(2)}) async-start(bf16[16,2,24,4,768]{4,2,1,3,0:T(8,128)(2,1)} %copy.40), calls=%async_computation.1 | async-start | bytes 9437184 | tf_op jit(solution)/shard_map/all_to_all | solution.py:27
  54.1 6.7 %copy.42 = bf16[4,768,768]{1,2,0:T(8,128)(2,1)} copy(bf16[4,768,768]{2,1,0:T(8,128)(2,1)} %param.12) | data formatting | bytes 9437184 | tf_op args[5]
  60.8 64.5 %all-to-all-done.1 = bf16[16,2,24,4,768]{4,2,1,3,0:T(8,128)(2,1)} async-done(((bf16[16,2,24,4,768]{4,2,1,3,0:T(8,128)(2,1)}), bf16[16,2,24,4,768]{4,2,1,3,0:T(8,128)(2,1)}, u32[]{:S(2)}, u32[]{:S(2)}) %all-to-all-start.1) | async-done | bytes 4718624 | tf_op jit(solution)/shard_map/all_to_all | solution.py:27
  125.2 8.4 %stack.22 = bf16[4,4,768,768]{2,3,1,0:T(8,128)(2,1)} broadcast(bf16[4,768,768]{1,2,0:T(8,128)(2,1)} %copy.42), dimensions={1,2,3} | broadcast | bytes 23592960 | tf_op jit(solution)/shard_map/stack | solution.py:71
  133.6 7.5 %all-to-all-start.2 = ((bf16[4,4,768,768]{2,3,1,0:T(8,128)(2,1)}), bf16[4,4,768,768]{2,3,1,0:T(8,128)(2,1)}, u32[]{:S(2)}, u32[]{:S(2)}) async-start(bf16[4,4,768,768]{2,3,1,0:T(8,128)(2,1)} %stack.22), calls=%async_computation.2 | async-start | bytes 37748736 | tf_op jit(solution)/shard_map/all_to_all | solution.py:71
  141.1 4.9 copy.41
  146.0 239.5 %all-to-all-done.2 = bf16[4,4,768,768]{2,3,1,0:T(8,128)(2,1)} async-done(((bf16[4,4,768,768]{2,3,1,0:T(8,128)(2,1)}), bf16[4,4,768,768]{2,3,1,0:T(8,128)(2,1)}, u32[]{:S(2)}, u32[]{:S(2)}) %all-to-all-start.2) | async-done | bytes 18874400 | tf_op jit(solution)/shard_map/all_to_all | solution.py:71
  385.5 17.1 %copy.43 = bf16[4,4,768,768]{2,3,0,1:T(8,128)(2,1)} copy(bf16[4,4,768,768]{2,3,1,0:T(8,128)(2,1)} %all-to-all-done.2) | data formatting | bytes 37748736 | tf_op jit(solution)/shard_map/all_to_all | solution.py:71
  402.6 4.1 convolution_convert_fusion.14
  406.7 5.2 convolution_convert_fusion.13
  411.9 5.2 convolution_convert_fusion.12
  417.1 4.1 convolution_convert_fusion.10
  421.2 5.2 convolution_convert_fusion.9
  426.4 5.1 convolution_convert_fusion.8
  431.5 5.2 convolution_convert_fusion.6
  436.7 5.2 convolution_convert_fusion.5
  441.9 5.4 convolution_convert_fusion.4
  447.3 5.1 convolution_convert_fusion.2
  452.4 5.1 convolution_convert_fusion.1
  457.5 5.1 convolution_convert_fusion
  462.7 4.9 add_convert_fusion.3
  467.6 5.0 add_convert_fusion.2
  472.6 5.2 add_convert_fusion.1
  477.8 6.5 %add_convert_fusion = bf16[768,768]{1,0:T(8,128)(2,1)} fusion(bf16[768,768]{1,0:T(8,128)(2,1)} %convolution_convert_fusion, bf16[768,768]{1,0:T(8,128)(2,1)} %convolution_convert_fusion.1, bf16[768,768]{1,0:T(8,128)(2,1)} %convolution_convert_fusion.2, bf16[4,3072,768]{2,1,0:T(8,128)(2,1)} %all-gather.2.cloned.1.call-done, ...), kind=kOutput, calls=%fused_computation.6 | convolution fusion | flops 1818427392 | bytes 8257536 | tf_op jit(solution)/shard_map/dot_general | solution.py:56
  484.4 1.7 pad_maximum_fusion
  486.1 0.3 copy.51
  486.4 7.5 %all_to_all.26 = bf16[16,2,24,4,768]{4,2,0,3,1:T(8,128)(2,1)S(1)} all-to-all(bf16[16,2,24,4,768]{4,2,0,3,1:T(8,128)(2,1)S(1)} %copy.51), channel_id=1, replica_groups=mesh['expert_0'=4,'expert_1'=4,'expert_2'=2,'helper'=4] {'expert_2'}, dimensions={1} | all-to-all | bytes 9437184 | tf_op jit(solution)/shard_map/all_to_all | solution.py:27
  493.9 0.5 copy.48
  494.4 63.6 %all_to_all.27 = bf16[16,2,24,4,768]{4,2,1,3,0:T(8,128)(2,1)S(1)} all-to-all(bf16[16,2,24,4,768]{4,2,1,3,0:T(8,128)(2,1)S(1)} %copy.48), channel_id=1, replica_groups=mesh['expert_0'=4,'expert_1'=4,'expert_2'=2,'helper'=4] {'expert_0','exp..., dimensions={0} | all-to-all | bytes 9437184 | tf_op jit(solution)/shard_map/all_to_all | solution.py:27
  558.0 0.6 copy.49
  558.6 3.2 copy.52
  561.7 14.3 %gather_fusion = bf16[1024,768]{1,0:T(8,128)(2,1)S(1)} fusion(bf16[24,128,768]{2,1,0:T(8,128)(2,1)} %copy.52, s32[1024]{0:T(1024)S(1)} %bitcast.233), kind=kCustom, calls=%fused_computation | custom fusion | bytes 3153920 | tf_op jit(solution)/shard_map/gather | solution.py:89
  576.1 1.5 multiply_convert_fusion
  (29 shorter events, 0.6 us)
Async XLA Ops:
  6.5 0.7 copy-start
  6.5 396.1 %all-gather.2.cloned.1.call-start = ((), (), s32[]{:S(2)}) async-start(), calls=%async_computation.5 | async-start | bytes 23592960 | tf_op jit(solution)/shard_map/all_gather | solution.py:73
  7.3 0.7 copy-start.3
  7.3 1.3 copy-start.1
  7.7 2.0 copy-start.5
  7.7 2.1 copy-start.4
  45.7 79.5 %all-to-all-start.1 = ((bf16[16,2,24,4,768]{4,2,1,3,0:T(8,128)(2,1)}), bf16[16,2,24,4,768]{4,2,1,3,0:T(8,128)(2,1)}, u32[]{:S(2)}, u32[]{:S(2)}) async-start(bf16[16,2,24,4,768]{4,2,1,3,0:T(8,128)(2,1)} %copy.40), calls=%async_computation.1 | async-start | bytes 9437184 | tf_op jit(solution)/shard_map/all_to_all | solution.py:27
  133.6 251.9 %all-to-all-start.2 = ((bf16[4,4,768,768]{2,3,1,0:T(8,128)(2,1)}), bf16[4,4,768,768]{2,3,1,0:T(8,128)(2,1)}, u32[]{:S(2)}, u32[]{:S(2)}) async-start(bf16[4,4,768,768]{2,3,1,0:T(8,128)(2,1)} %stack.22), calls=%async_computation.2 | async-start | bytes 37748736 | tf_op jit(solution)/shard_map/all_to_all | solution.py:71
  561.7 14.3 %copy-start.2 = (f32[1024]{0:T(1024)S(1)}, f32[1024]{0:T(1024)}, u32[]{:S(2)}) copy-start(f32[1024]{0:T(1024)} %param.8) | copy-start | bytes 12292
Sparse Core Ops, SparseCore 0:
  9.0 212.6 all-gather.1
